TPU v7x, 512 devices: a whole 4x4x16 slice. The times are simulated.
512 devices in a mesh: row: 16 (over z), col: 16 (over y, x_lo, core), depth: 2 (over x_hi).
Axes of the slice: x: 4 (x_hi: 2, x_lo: 2; x = x_hi * 2 + x_lo), y: 4, z: 16, core: 2. Of those that a mesh axis runs over, the one named last changes fastest.
Arguments:
- amplitudes: float32 [3072, 11520], P('row', ('col', 'depth')), may hold values from -6 to 6
- integrals: float32 [11520, 5760], P(('row', 'depth'), 'col'), may hold values from -0.0546875 to 0.0546875
Outputs:
- ladder: float32 [3072, 5760], P(('row', 'depth'), 'col')
All inputs are finite; a program needn't handle non-finite values.
Results may differ from a plain program's by a relative error of at most 0.00007.
Values sent between devices are 32-bit elements; how exact they have to be, the bound alone decides.
No kernel may reach another device: no remote copies, remote signals or barrier semaphores. Data moves between devices by JAX's collectives and lax.ppermute only.
A program may use at most 64 MiB of HBM per device.

v0:
```python
import jax
import jax.numpy as jnp
from jax import lax
from jax.sharding import PartitionSpec as P


def local(amplitudes, integrals):
    slab = lax.all_gather(integrals, "row", axis=0, tiled=True)
    total = jnp.dot(
        lax.all_gather(amplitudes, "col", axis=1, tiled=True),
        slab,
        precision=lax.Precision.HIGHEST,
        preferred_element_type=jnp.float32,
    )
    return lax.psum_scatter(0.5 * total, "depth", scatter_dimension=0, tiled=True)


def solution(mesh):
    placed = (P("row", ("col", "depth")), P(("row", "depth"), "col"))
    return jax.shard_map(
        local, mesh=mesh, in_specs=placed, out_specs=P(("row", "depth"), "col"), check_vma=False
    )
```

profile of v0, /device:TPU:1, one launch (start us, length us, event | category | flops | bytes accessed | tf_op | source)
XLA Modules:
  0.0 213.8 jit_solution(3228303676502207377)
XLA Ops:
  6.5 0.0 all-gather.6.cloned.1.call-start
  6.5 0.7 all-gather.6.cloned.1.call-update
  7.3 0.0 all-gather.4.cloned.1.call-start
  7.3 0.7 all-gather.4.cloned.1.call-update
  8.0 0.0 reduce-scatter.2.cloned.1.call-start
  8.1 53.4 %all-gather.6.cloned.1.call-done = f32[16,360,192]{1,2,0:T(8,128)} async-done(((f32[1,360,192]{1,2,0:T(8,128)}), f32[16,360,192]{1,2,0:T(8,128)}) %all-gather.6.cloned.1.call-update) | async-done | bytes 4423696 | tf_op jit(solution)/shard_map/all_gather | solution.py:10
  61.5 7.2 %copy.4 = f32[16,360,192]{1,0,2:T(8,128)} copy(f32[16,360,192]{1,2,0:T(8,128)} %all-gather.6.cloned.1.call-done) | data formatting | bytes 8847360 | tf_op jit(solution)/shard_map/all_gather | solution.py:10
  68.7 5.9 %reshape.1 = f32[5760,192]{0,1:T(8,128)} reshape(f32[16,360,192]{1,0,2:T(8,128)} %copy.4) | data formatting | bytes 8847360
  74.5 99.1 %all-gather.4.cloned.1.call-done = f32[5760,360]{1,0:T(8,128)} async-done(((f32[360,360]{1,0:T(8,128)}), f32[5760,360]{1,0:T(8,128)}) %all-gather.4.cloned.1.call-update) | async-done | bytes 8294416 | tf_op jit(solution)/shard_map/all_gather | solution.py:8
  173.6 11.8 %convolution_multiply_fusion = f32[192,360]{1,0:T(8,128)} fusion(f32[5760,192]{0,1:T(8,128)} %reshape.1, f32[5760,360]{1,0:T(8,128)} %all-gather.4.cloned.1.call-done), kind=kOutput, calls=%fused_computation | convolution fusion | flops 4777643520 | bytes 12994560 | tf_op jit(solution)/shard_map/dot_general | solution.py:9
  185.4 0.0 reduce-scatter.2.cloned.1.call-update
  185.5 21.8 %reduce-scatter.2.cloned.1.call-done = f32[96,360]{1,0:T(8,128)} async-done(((f32[192,360]{1,0:T(8,128)}), f32[96,360]{1,0:T(8,128)}) %reduce-scatter.2.cloned.1.call-update) | async-done | bytes 138256 | tf_op jit(solution)/shard_map/reduce_scatter | solution.py:15
Async XLA Ops:
  6.5 54.9 %all-gather.6.cloned.1.call-start = ((), (), s32[]{:S(2)}) async-start(), calls=%async_computation.3 | async-start | bytes 5013504 | tf_op jit(solution)/shard_map/all_gather | solution.py:10
  7.3 166.4 %all-gather.4.cloned.1.call-start = ((), (), s32[]{:S(2)}) async-start(), calls=%async_computation.1 | async-start | bytes 9400320 | tf_op jit(solution)/shard_map/all_gather | solution.py:8
  8.0 199.3 %reduce-scatter.2.cloned.1.call-start = ((), (), s32[]{:S(2)}) async-start(), calls=%async_computation.2 | async-start | bytes 442368 | tf_op jit(solution)/shard_map/reduce_scatter | solution.py:15
Sparse Core Ops, SparseCore 0:
  9.5 51.9 all-gather.5
  63.6 110.0 all-gather.3
  185.6 21.6 reduce-scatter.1
where the time goes:
time: 214 us
  waiting for transfers between devices  176 us (82%)
  local copies, waits for them, and re-layouts  13.1 us (6%)
  between operations  13.1 us (6%)
  matrix products  11.8 us (6%)
    all_gather x1, waiting for transfers between devices, local(): slab = lax.all_gather(integrals, 'row', axis=0, tiled=True)  99.1 us
    all_gather x1, waiting for transfers between devices, local(): lax.all_gather(amplitudes, 'col', axis=1, tiled=True)  53.4 us
    reduce_scatter x1, waiting for transfers between devices, local(): lax.psum_scatter(0.5 * total, 'depth', scatter_dimension=0, tiled=True)  21.8 us
    dot_general x1, matrix products, local(): jnp.dot(lax.all_gather(amplitudes, 'col', axis=1, tiled=True), slab, prec...  11.8 us
    all_gather x1, local copies, waits for them, and re-layouts, local(): lax.all_gather(amplitudes, 'col', axis=1, tiled=True)  7.19 us
    unnamed x1, local copies, waits for them, and re-layouts  5.87 us
  transfers between devices with their start and end apart: 3, of which 3 were waited for; matrix products, arithmetic and copies ran while one was open for 6% of the time, Pallas kernels for 0%

commit v1 on v0

--- a/solution.py
+++ b/solution.py
@@ -5,7 +5,9 @@
 
 
 def local(amplitudes, integrals):
-    slab = lax.all_gather(integrals, "row", axis=0, tiled=True)
+    slab = jnp.concatenate(
+        lax.all_to_all(jnp.stack([integrals] * lax.axis_size("row")), "row", 0, 0), axis=0
+    )
     total = jnp.dot(
         lax.all_gather(amplitudes, "col", axis=1, tiled=True),
         slab,

time: 214 us -> 452 us (2.11)
  waiting for transfers between devices: 176 us -> 393 us
  starting transfers between devices: 0.08 us -> 15.9 us
  local copies, waits for them, and re-layouts: 13.1 us -> 18.1 us
    all_to_all x0 -> x1, waiting for transfers between devices: none -> 317 us  [local(): lax.all_to_all(jnp.stack([integrals] * lax.axis_size('row')), 'row', 0, 0)]
    all_gather x1 -> x0, waiting for transfers between devices: 99.1 us -> none  [local(): slab = lax.all_gather(integrals, 'row', axis=0, tiled=True)]
    all_to_all x0 -> x1, starting transfers between devices: none -> 15.8 us  [local(): lax.all_to_all(jnp.stack([integrals] * lax.axis_size('row')), 'row', 0, 0)]
    another operation x0 -> x1, local copies, waits for them, and re-layouts: none -> 5.06 us  [local(): jnp.stack([integrals] * lax.axis_size('row'))]
  transfers between devices with their start and end apart: 3 -> 3, of which waited for: 3 -> 3; matrix products, arithmetic and copies ran while one was open for 6% -> 3% of each run, Pallas kernels for 0% -> 0%
where the time goes in v1:
time: 452 us
  waiting for transfers between devices  393 us (87%)
  local copies, waits for them, and re-layouts  18.1 us (4%)
  starting transfers between devices  15.9 us (4%)
  between operations  13.4 us (3%)
  matrix products  11.8 us (3%)
    all_to_all x1, waiting for transfers between devices, local(): lax.all_to_all(jnp.stack([integrals] * lax.axis_size('row')), 'row', 0, 0)  317 us
    all_gather x1, waiting for transfers between devices, local(): lax.all_gather(amplitudes, 'col', axis=1, tiled=True)  50.3 us
    reduce_scatter x1, waiting for transfers between devices, local(): lax.psum_scatter(0.5 * total, 'depth', scatter_dimension=0, tiled=True)  24.6 us
    all_to_all x1, starting transfers between devices, local(): lax.all_to_all(jnp.stack([integrals] * lax.axis_size('row')), 'row', 0, 0)  15.8 us
    dot_general x1, matrix products, local(): jnp.dot(lax.all_gather(amplitudes, 'col', axis=1, tiled=True), slab, prec...  11.8 us
  transfers between devices with their start and end apart: 3, of which 3 were waited for; matrix products, arithmetic and copies ran while one was open for 3% of the time, Pallas kernels for 0%

profile of v1, /device:TPU:1, one launch (start us, length us, event | category | flops | bytes accessed | tf_op | source)
XLA Modules:
  0.0 451.9 jit_solution(7981550543094723309)
XLA Ops:
  6.5 5.1 %stack.2 = f32[16,360,360]{2,1,0:T(8,128)} broadcast(f32[360,360]{1,0:T(8,128)} %param.3), dimensions={1,2} | broadcast | bytes 8812800 | tf_op jit(solution)/shard_map/stack | solution.py:9
  11.6 15.8 %all-to-all-start = ((f32[16,360,360]{2,1,0:T(8,128)}), f32[16,360,360]{2,1,0:T(8,128)}, u32[]{:S(2)}, u32[]{:S(2)}) async-start(f32[16,360,360]{2,1,0:T(8,128)} %stack.2), calls=%async_computation | async-start | bytes 17694720 | tf_op jit(solution)/shard_map/all_to_all | solution.py:9
  27.4 0.0 all-gather.3.cloned.1.call-start
  27.4 0.7 all-gather.3.cloned.1.call-update
  28.1 0.0 reduce-scatter.2.cloned.1.call-start
  28.2 50.3 %all-gather.3.cloned.1.call-done = f32[16,360,192]{1,2,0:T(8,128)} async-done(((f32[1,360,192]{1,2,0:T(8,128)}), f32[16,360,192]{1,2,0:T(8,128)}) %all-gather.3.cloned.1.call-update) | async-done | bytes 4423696 | tf_op jit(solution)/shard_map/all_gather | solution.py:12
  78.5 7.2 %copy.4 = f32[16,360,192]{1,0,2:T(8,128)} copy(f32[16,360,192]{1,2,0:T(8,128)} %all-gather.3.cloned.1.call-done) | data formatting | bytes 8847360 | tf_op jit(solution)/shard_map/all_gather | solution.py:12
  85.7 5.8 %reshape.7 = f32[5760,192]{0,1:T(8,128)} reshape(f32[16,360,192]{1,0,2:T(8,128)} %copy.4) | data formatting | bytes 8847360
  91.5 317.1 %all-to-all-done = f32[16,360,360]{2,1,0:T(8,128)} async-done(((f32[16,360,360]{2,1,0:T(8,128)}), f32[16,360,360]{2,1,0:T(8,128)}, u32[]{:S(2)}, u32[]{:S(2)}) %all-to-all-start) | async-done | bytes 8294432 | tf_op jit(solution)/shard_map/all_to_all | solution.py:9
  408.6 11.8 %convolution_multiply_fusion = f32[192,360]{1,0:T(8,128)} fusion(f32[5760,192]{0,1:T(8,128)} %reshape.7, f32[5760,360]{1,0:T(8,128)} %bitcast.2), kind=kOutput, calls=%fused_computation | convolution fusion | flops 4777643520 | bytes 12994560 | tf_op jit(solution)/shard_map/dot_general | solution.py:11
  420.4 0.0 reduce-scatter.2.cloned.1.call-update
  420.5 24.6 %reduce-scatter.2.cloned.1.call-done = f32[96,360]{1,0:T(8,128)} async-done(((f32[192,360]{1,0:T(8,128)}), f32[96,360]{1,0:T(8,128)}) %reduce-scatter.2.cloned.1.call-update) | async-done | bytes 138256 | tf_op jit(solution)/shard_map/reduce_scatter | solution.py:17
Async XLA Ops:
  11.6 397.0 %all-to-all-start = ((f32[16,360,360]{2,1,0:T(8,128)}), f32[16,360,360]{2,1,0:T(8,128)}, u32[]{:S(2)}, u32[]{:S(2)}) async-start(f32[16,360,360]{2,1,0:T(8,128)} %stack.2), calls=%async_computation | async-start | bytes 17694720 | tf_op jit(solution)/shard_map/all_to_all | solution.py:9
  27.4 51.1 %all-gather.3.cloned.1.call-start = ((), (), s32[]{:S(2)}) async-start(), calls=%async_computation.3 | async-start | bytes 5013504 | tf_op jit(solution)/shard_map/all_gather | solution.py:12
  28.1 416.9 %reduce-scatter.2.cloned.1.call-start = ((), (), s32[]{:S(2)}) async-start(), calls=%async_computation.2 | async-start | bytes 442368 | tf_op jit(solution)/shard_map/reduce_scatter | solution.py:17
Sparse Core Ops, SparseCore 0:
  30.4 48.0 all-gather.2
  420.6 24.4 reduce-scatter.1
